TPU v7x, 256 devices: a whole 4x4x8 slice. The times are simulated.
256 devices in a mesh: context: 16 (over z, core), heads: 16 (over x, y).
Axes of the slice: x: 4, y: 4, z: 8, core: 2. Of those that a mesh axis runs over, the one named last changes fastest.
Arguments:
- main_query: bfloat16 [256, 128, 576], P('context', 'heads'), may hold values from -6 to 6
- latent_keys: bfloat16 [32768, 576], P('context'), may hold values from -6 to 6
- head_lse: float32 [256, 128], P(None, 'heads'), may hold values from 4 to 8
- lengths: int32 [256], replicated, may hold values from 1 to 32768, as said below
- index_query: bfloat16 [256, 64, 128], P('heads'), may hold values from -256 to 256
- index_key: bfloat16 [32768, 128], P('context'), may hold values from -8 to 8
- index_weight: float32 [256, 64], P('heads'), may hold values from -2.4 to 2.4
Outputs:
- grad_index_query: float32 [256, 64, 128], P('heads', 'context')
- grad_index_key: float32 [32768, 128], P(('context', 'heads'))
Inputs may be any that keep to these rules, and one draw needn't show every extreme that they name: Query rows come in blocks of 16 consecutive rows whose lengths rise by one from row to row; some block ends at the last key.
All inputs are finite; a program needn't handle non-finite values.
Results may differ from a plain program's by a relative error of at most 0.0029.
Values may be sent and summed in bfloat16 or wider, within the bound.
A program may use at most 64 MiB of HBM per device.

v0:
```python
import math
import jax
import jax.numpy as jnp
from jax import lax
from jax.sharding import PartitionSpec as P

main_scale = 192.0 ** (-0.5)
loss_scale = 64.0
masked_low = -1e30


def head_mass(queries, lse_rows, len_rows, latent, first_key):
    row_count = queries.shape[0]
    block_rows = math.gcd(row_count, 64)
    steps_count = row_count // block_rows
    key_pos = first_key + jnp.arange(latent.shape[0], dtype=jnp.int32)

    def one_block(inputs):
        query_block, lse_block, len_block = inputs
        scores = (
            jnp.einsum("rhd,sd->rhs", query_block, latent, preferred_element_type=jnp.float32)
            * main_scale
        )
        summed = jnp.sum(jnp.exp(scores - lse_block[:, :, None]), axis=1)
        return jnp.where(key_pos[None, :] < len_block[:, None], summed, 0.0)

    stacked = lax.map(
        one_block,
        (
            queries.reshape((steps_count, block_rows) + queries.shape[1:]),
            lse_rows.reshape(steps_count, block_rows, lse_rows.shape[1]),
            len_rows.reshape(steps_count, block_rows),
        ),
    )
    return stacked.reshape(row_count, latent.shape[0])


def on_device(main_query, latent_keys, head_lse, lengths, index_query, index_key, index_weight):
    key_count = latent_keys.shape[0]
    first_key = lax.axis_index("context") * key_count
    own_rows = index_query.shape[0]
    row_first = lax.axis_index("heads") * own_rows
    partial_mass = head_mass(
        lax.all_gather(main_query, "context", axis=0, tiled=True),
        head_lse,
        lengths,
        latent_keys,
        first_key,
    )
    summed_mass = lax.psum(partial_mass, "heads")
    row_mass = lax.dynamic_slice_in_dim(summed_mass, row_first, own_rows, 0)
    own_len = lax.dynamic_slice_in_dim(lengths, row_first, own_rows, 0)
    visible = (first_key + jnp.arange(key_count, dtype=jnp.int32))[None, :] < own_len[:, None]
    heads_count = index_query.shape[1]
    width = index_query.shape[2]
    index_scale = width ** (-0.5)
    flat_query = index_query.reshape(own_rows * heads_count, width)
    block_keys = math.gcd(key_count, 512)
    block_total = key_count // block_keys
    key_blocks = index_key.reshape(block_total, block_keys, width)

    def block_dots(key_block):
        products = lax.dot_general(
            flat_query, key_block, (((1,), (1,)), ((), ())), preferred_element_type=jnp.float32
        )
        return products.reshape(own_rows, heads_count, key_block.shape[0])

    def block_logits(key_block):
        return (
            jnp.einsum(
                "tj,tjs->ts",
                index_weight,
                jax.nn.relu(block_dots(key_block)),
                precision=lax.Precision.HIGHEST,
            )
            * index_scale
        )

    logits = jnp.moveaxis(lax.map(block_logits, key_blocks), 0, 1).reshape(own_rows, key_count)
    local_top = jnp.max(jnp.where(visible, logits, masked_low), axis=1)
    mass_local = jnp.sum(row_mass, axis=1)
    top = lax.pmax(local_top, "context")
    weights_exp = jnp.where(visible, jnp.exp(logits - top[:, None]), 0.0)
    share_sum, mass_total = lax.psum((jnp.sum(weights_exp, axis=1), mass_local), "context")
    probability = weights_exp / share_sum[:, None]
    target = row_mass / mass_total[:, None]
    slopes = loss_scale * (probability - target)
    slope_blocks = slopes.reshape(own_rows, block_total, block_keys).transpose(1, 0, 2)

    def back_step(query_grad, inputs):
        key_block, slope_block = inputs
        products = block_dots(key_block)
        terms = jnp.where(
            products > 0, slope_block[:, None, :] * index_weight[:, :, None] * index_scale, 0.0
        )
        terms = terms.astype(jnp.bfloat16).reshape(own_rows * heads_count, key_block.shape[0])
        query_grad = query_grad + jnp.dot(terms, key_block, preferred_element_type=jnp.float32)
        key_grad = lax.dot_general(
            terms, flat_query, (((0,), (0,)), ((), ())), preferred_element_type=jnp.float32
        )
        return (query_grad, key_grad)

    start_grad = jnp.zeros((own_rows * heads_count, width), jnp.float32)
    query_grad, key_grads = lax.scan(back_step, start_grad, (key_blocks, slope_blocks))
    query_grad = query_grad.reshape(own_rows, heads_count, width)
    key_grad = key_grads.reshape(key_count, width)
    out_query = lax.psum_scatter(query_grad, "context", scatter_dimension=1, tiled=True)
    out_key = lax.psum_scatter(key_grad, "heads", scatter_dimension=0, tiled=True)
    return (out_query, out_key)


def solution(mesh):
    placed = (
        P("context", "heads", None),
        P("context", None),
        P(None, "heads"),
        P(),
        P("heads", None, None),
        P("context", None),
        P("heads", None),
    )
    return jax.shard_map(
        on_device,
        mesh=mesh,
        in_specs=placed,
        out_specs=(P("heads", "context", None), P(("context", "heads"), None)),
        check_vma=False,
    )
```

profile of v0, /device:TPU:2, one launch (start us, length us, event | category | flops | bytes accessed | tf_op | source)
XLA Modules:
  0.0 374.9 jit_solution(15053279912884742428)
XLA Ops:
  11.1 41.8 %all-gather.2.cloned.1.call-done = bf16[256,8,576]{2,1,0:T(8,128)(2,1)} async-done(((bf16[16,8,576]{2,1,0:T(8,128)(2,1)}), bf16[256,8,576]{2,1,0:T(8,128)(2,1)}) %all-gather.2.cloned.1.call-update) | async-done | bytes 2359312 | tf_op jit(solution)/shard_map/all_gather | solution.py:44
  52.9 22.9 %while.36 = (s32[]{:T(128)}, f32[4,64,2048]{2,1,0:T(8,128)}, s32[4,64]{1,0:T(4,128)S(1)}, bf16[4,64,8,576]{3,2,1,0:T(8,128)(2,1)}, bf16[2048,576]{0,1:T(8,128)(2...) while((s32[]{:T(128)}, f32[4,64,2048]{2,1,0:T(8,128)}, s32[4,64]{1,0:T(4,128)S(1)}, ...), condition=%wide.region_8.9_spmd.clone, body=%wide.region_6.8_spmd.clone.sunk | while | flops 1211238400 | bytes 4611937 | solution.py:27
  52.9 4.8 %exponential_reduce_fusion.2 = f32[64,2048]{1,0:T(8,128)S(1)} fusion(bf16[2048,576]{0,1:T(8,128)(2,1)} %get-tuple-element.382, f32[64,8]{1,0:T(8,128)S(1)} %dynamic-slice_bitcast_fusion.5, bf16[4,64,8,576]{3,2,1,0:T(8,128)(2,1)} %get-tuple-element.381, s32[]{:T(128)} %get-tuple-element.370), kind=kOutput, calls=%fused_computation.7.clone.1 | convolution fusion | flops 1210974208 | bytes 3541504 | tf_op jit(solution)/shard_map/while/body/eval_jaxpr/rhd,sd->rhs/dot_general | solution.py:21
  58.6 4.8 %exponential_reduce_fusion.2 = f32[64,2048]{1,0:T(8,128)S(1)} fusion(bf16[2048,576]{0,1:T(8,128)(2,1)} %get-tuple-element.382, f32[64,8]{1,0:T(8,128)S(1)} %dynamic-slice_bitcast_fusion.5, bf16[4,64,8,576]{3,2,1,0:T(8,128)(2,1)} %get-tuple-element.381, s32[]{:T(128)} %get-tuple-element.370), kind=kOutput, calls=%fused_computation.7.clone.1 | convolution fusion | flops 1210974208 | bytes 3541504 | tf_op jit(solution)/shard_map/while/body/eval_jaxpr/rhd,sd->rhs/dot_general | solution.py:21
  64.3 4.8 %exponential_reduce_fusion.2 = f32[64,2048]{1,0:T(8,128)S(1)} fusion(bf16[2048,576]{0,1:T(8,128)(2,1)} %get-tuple-element.382, f32[64,8]{1,0:T(8,128)S(1)} %dynamic-slice_bitcast_fusion.5, bf16[4,64,8,576]{3,2,1,0:T(8,128)(2,1)} %get-tuple-element.381, s32[]{:T(128)} %get-tuple-element.370), kind=kOutput, calls=%fused_computation.7.clone.1 | convolution fusion | flops 1210974208 | bytes 3541504 | tf_op jit(solution)/shard_map/while/body/eval_jaxpr/rhd,sd->rhs/dot_general | solution.py:21
  70.0 4.8 %exponential_reduce_fusion.2 = f32[64,2048]{1,0:T(8,128)S(1)} fusion(bf16[2048,576]{0,1:T(8,128)(2,1)} %get-tuple-element.382, f32[64,8]{1,0:T(8,128)S(1)} %dynamic-slice_bitcast_fusion.5, bf16[4,64,8,576]{3,2,1,0:T(8,128)(2,1)} %get-tuple-element.381, s32[]{:T(128)} %get-tuple-element.370), kind=kOutput, calls=%fused_computation.7.clone.1 | convolution fusion | flops 1210974208 | bytes 3541504 | tf_op jit(solution)/shard_map/while/body/eval_jaxpr/rhd,sd->rhs/dot_general | solution.py:21
  76.9 19.8 %while.35 = (s32[]{:T(128)}, f32[4,16,512]{2,1,0:T(8,128)S(1)}, bf16[4,512,128]{2,1,0:T(8,128)(2,1)S(1)}, bf16[1024,128]{1,0:T(8,128)(2,1)S(1)}, f32[16,64]{1,0:T(8,128)S(1)}, /*index=5*/s32[]{:T(128)}) while((s32[]{:T(128)}, f32[4,16,512]{2,1,0:T(8,128)S(1)}, bf16[4,512,128]{2,1,0:T(8,128)(2,1)S(1)}, bf16[1024,128]{1,0:T(8,128)(2,1)S(1)}, ...), condition=%wide.region_1.2_spmd, body=%wide.region_0.1_spmd.sunk | while | flops 141041664 | bytes 8884301 | solution.py:79
  76.9 1.8 maximum_bitcast_fusion.2
  78.7 1.9 copy.41
  81.8 1.8 maximum_bitcast_fusion.2
  83.6 1.9 copy.41
  85.6 1.2 fusion.56
  86.8 1.8 maximum_bitcast_fusion.2
  88.6 1.9 copy.41
  90.5 1.2 fusion.56
  91.8 1.8 maximum_bitcast_fusion.2
  93.6 1.9 copy.41
  97.0 24.9 %pmax.7 = f32[16]{0:T(128)S(1)} all-reduce(f32[16]{0:T(128)S(1)} %fusion.18), channel_id=1, replica_groups=mesh['context'=16,'heads'=16] {'context'}, use_global_device_ids=true, to_apply=%region_3.4 | all-reduce | flops 16 | bytes 128 | tf_op jit(solution)/shard_map/pmax | solution.py:82
  122.1 53.3 %all-reduce.3.cloned.1.call-done = f32[256,2048]{1,0:T(8,128)} async-done(((f32[256,2048]{1,0:T(8,128)}), f32[256,2048]{1,0:T(8,128)}) %all-reduce.3.cloned.1.call-update) | async-done | bytes 2097168 | tf_op jit(solution)/shard_map/psum | solution.py:50
  176.4 24.2 %all-reduce = (f32[16]{0:T(128)S(1)}, f32[16]{0:T(128)S(1)}) all-reduce(f32[16]{0:T(128)S(1)} %dynamic-slice_reduce_fusion, f32[16]{0:T(128)S(1)} %fusion.19), channel_id=1, replica_groups=mesh['context'=16,'heads'=16] {'context'}, use_global_device_ids=true, to_apply=%region_11.12 | all-reduce | flops 32 | bytes 256 | tf_op jit(solution)/shard_map/psum | solution.py:84
  202.3 26.9 %while.37 = (s32[]{:T(128)}, f32[1024,128]{1,0:T(8,128)S(1)}, f32[4,512,128]{2,1,0:T(8,128)}, bf16[4,512,128]{2,1,0:T(8,128)(2,1)S(1)}, bf16[1024,128]{1,0:T(8,1...) while((s32[]{:T(128)}, f32[1024,128]{1,0:T(8,128)S(1)}, ...), condition=%wide.wide.region_13.14_spmd.clone, body=%wide.wide.region_12.13_spmd.clone.sunk | while | flops 405536768 | bytes 13734523 | solution.py:104
  203.3 1.8 copy.42
  205.2 2.1 select_convert_fusion.3
  210.0 1.8 copy.42
  211.9 2.1 select_convert_fusion.3
  216.8 1.8 copy.42
  218.6 2.1 select_convert_fusion.3
  223.5 1.8 copy.42
  225.3 2.1 select_convert_fusion.3
  231.0 56.1 %reduce-scatter.3.cloned.1.call-done = f32[16,4,128]{2,0,1:T(8,128)} async-done(((f32[16,64,128]{2,0,1:T(8,128)}), f32[16,4,128]{2,0,1:T(8,128)}) %reduce-scatter.3.cloned.1.call-update) | async-done | bytes 32784 | tf_op jit(solution)/shard_map/reduce_scatter | solution.py:107
  287.1 1.4 copy.28
  288.5 79.9 %reduce-scatter.5.cloned.1.call-done = f32[128,128]{1,0:T(8,128)} async-done(((f32[2048,128]{1,0:T(8,128)}), f32[128,128]{1,0:T(8,128)}) %reduce-scatter.5.cloned.1.call-update) | async-done | bytes 65552 | tf_op jit(solution)/shard_map/reduce_scatter | solution.py:108
  (69 shorter events, 27.2 us)
Async XLA Ops:
  7.2 45.7 %all-gather.2.cloned.1.call-start = ((), (), s32[]{:S(2)}) async-start(), calls=%async_computation.2 | async-start | bytes 2785280 | tf_op jit(solution)/shard_map/all_gather | solution.py:44
  7.9 167.5 %all-reduce.3.cloned.1.call-start = ((), (), s32[]{:S(2)}) async-start(), calls=%async_computation.3 | async-start | bytes 4194304 | tf_op jit(solution)/shard_map/psum | solution.py:50
  75.8 0.9 copy-start
  75.8 1.1 copy-start.1
  75.8 1.1 copy-start.2
  75.8 211.3 %reduce-scatter.3.cloned.1.call-start = ((), (), s32[]{:S(2)}) async-start(), calls=%async_computation.4 | async-start | bytes 557056 | tf_op jit(solution)/shard_map/reduce_scatter | solution.py:107
  230.4 138.0 %reduce-scatter.5.cloned.1.call-start = ((), (), s32[]{:S(2)}) async-start(), calls=%async_computation.5 | async-start | bytes 1114112 | tf_op jit(solution)/shard_map/reduce_scatter | solution.py:108
Sparse Core Ops, SparseCore 0:
  9.8 43.0 all-gather.1
  75.9 99.3 all-reduce.2
  230.5 56.5 reduce-scatter.2
  291.0 77.3 reduce-scatter.4
where the time goes:
time: 376 us; the launch traced here: 375 us
  waiting for transfers between devices  232 us (62%)
  blocking collectives  49.1 us (13%)
  matrix products  46.5 us (12%)
  local copies, waits for them, and re-layouts  26.4 us (7%)
  between operations  13.8 us (4%)
  other arithmetic  6.2 us (2%)
    reduce_scatter x1, waiting for transfers between devices, on_device(): lax.psum_scatter(key_grad, 'heads', scatter_dimension=0, tiled=True)  79.9 us
    reduce_scatter x1, waiting for transfers between devices, on_device(): lax.psum_scatter(query_grad, 'context', scatter_dimension=1, tiled=True)  56.1 us
    psum x1, waiting for transfers between devices, on_device(): summed_mass = lax.psum(partial_mass, 'heads')  53.3 us
    all_gather x1, waiting for transfers between devices, on_device(): lax.all_gather(main_query, 'context', axis=0, tiled=True)  41.8 us
    pmax x1, blocking collectives, on_device(): top = lax.pmax(local_top, 'context')  24.9 us
    psum x1, blocking collectives, on_device(): lax.psum((jnp.sum(weights_exp, axis=1), mass_local), 'context')  24.2 us
    dot_general x4, matrix products, one_block(): jnp.einsum('rhd,sd->rhs', query_block, latent, preferred_element_type=jnp...  19 us
    dot_general x8, matrix products, block_dots(): lax.dot_general(flat_query, key_block, (((1,), (1,)), ((), ())), preferre...  15.5 us
  transfers between devices with their start and end apart: 4, of which 4 were waited for; matrix products, arithmetic and copies ran while one was open for 7% of the time, Pallas kernels for 0%

commit v1 on v0

--- a/solution.py
+++ b/solution.py
@@ -41,7 +41,10 @@
     own_rows = index_query.shape[0]
     row_first = lax.axis_index("heads") * own_rows
     partial_mass = head_mass(
-        lax.all_gather(main_query, "context", axis=0, tiled=True),
+        jnp.concatenate(
+            lax.all_to_all(jnp.stack([main_query] * lax.axis_size("context")), "context", 0, 0),
+            axis=0,
+        ),
         head_lse,
         lengths,
         latent_keys,

time: 376 us -> 400 us (1.064)
  waiting for transfers between devices: 232 us -> 251 us
  starting transfers between devices: 0.16 us -> 8.88 us
    all_to_all x0 -> x1, waiting for transfers between devices: none -> 60.1 us  [on_device(): lax.all_to_all(jnp.stack([main_query] * lax.axis_size('context')), 'conte...]
    all_gather x1 -> x0, waiting for transfers between devices: 41.8 us -> none  [on_device(): lax.all_gather(main_query, 'context', axis=0, tiled=True)]
    all_to_all x0 -> x1, starting transfers between devices: none -> 8.76 us  [on_device(): lax.all_to_all(jnp.stack([main_query] * lax.axis_size('context')), 'conte...]
  transfers between devices with their start and end apart: 4 -> 4, of which waited for: 4 -> 4; matrix products, arithmetic and copies ran while one was open for 7% -> 5% of each run, Pallas kernels for 0% -> 0%
where the time goes in v1:
time: 400 us; the launch traced here: 399 us
  waiting for transfers between devices  251 us (63%)
  blocking collectives  48.6 us (12%)
  matrix products  43.1 us (11%)
  local copies, waits for them, and re-layouts  26.6 us (7%)
  between operations  13.9 us (3%)
  starting transfers between devices  8.88 us (2%)
  other arithmetic  6.21 us (2%)
    reduce_scatter x1, waiting for transfers between devices, on_device(): lax.psum_scatter(key_grad, 'heads', scatter_dimension=0, tiled=True)  80 us
    all_to_all x1, waiting for transfers between devices, on_device(): lax.all_to_all(jnp.stack([main_query] * lax.axis_size('context')), 'conte...  60.1 us
    reduce_scatter x1, waiting for transfers between devices, on_device(): lax.psum_scatter(query_grad, 'context', scatter_dimension=1, tiled=True)  56 us
    psum x1, waiting for transfers between devices, on_device(): summed_mass = lax.psum(partial_mass, 'heads')  54.5 us
    pmax x1, blocking collectives, on_device(): top = lax.pmax(local_top, 'context')  24.4 us
    psum x1, blocking collectives, on_device(): lax.psum((jnp.sum(weights_exp, axis=1), mass_local), 'context')  24.2 us
    dot_general x4, matrix products, one_block(): jnp.einsum('rhd,sd->rhs', query_block, latent, preferred_element_type=jnp...  15.9 us
    dot_general x8, matrix products, block_dots(): lax.dot_general(flat_query, key_block, (((1,), (1,)), ((), ())), preferre...  15.3 us
  transfers between devices with their start and end apart: 4, of which 4 were waited for; matrix products, arithmetic and copies ran while one was open for 5% of the time, Pallas kernels for 0%

profile of v1, /device:TPU:2, one launch (start us, length us, event | category | flops | bytes accessed | tf_op | source)
XLA Modules:
  0.0 398.8 jit_solution(3548400001475974303)
XLA Ops:
  7.2 2.8 stack.2
  9.9 8.8 %all-to-all-start = ((bf16[16,16,8,576]{3,2,1,0:T(8,128)(2,1)}), bf16[16,16,8,576]{3,2,1,0:T(8,128)(2,1)}, u32[]{:S(2)}, u32[]{:S(2)}) async-start(bf16[16,16,8,576]{3,2,1,0:T(8,128)(2,1)} %stack.2), calls=%async_computation | async-start | bytes 5242880 | tf_op jit(solution)/shard_map/all_to_all | solution.py:45
  19.2 60.1 %all-to-all-done = bf16[16,16,8,576]{3,2,1,0:T(8,128)(2,1)} async-done(((bf16[16,16,8,576]{3,2,1,0:T(8,128)(2,1)}), bf16[16,16,8,576]{3,2,1,0:T(8,128)(2,1)}, u32[]{:S(2)}, u32[]{:S(2)}) %all-to-all-start) | async-done | bytes 2359328 | tf_op jit(solution)/shard_map/all_to_all | solution.py:45
  79.3 19.8 %while.36 = (s32[]{:T(128)}, f32[4,64,2048]{2,1,0:T(8,128)}, s32[4,64]{1,0:T(4,128)S(1)}, bf16[4,64,8,576]{3,2,1,0:T(8,128)(2,1)}, bf16[2048,576]{0,1:T(8,128)(2...) while((s32[]{:T(128)}, f32[4,64,2048]{2,1,0:T(8,128)}, s32[4,64]{1,0:T(4,128)S(1)}, ...), condition=%wide.region_8.9_spmd.clone, body=%wide.region_6.8_spmd.clone.sunk | while | flops 1211238400 | bytes 4611937 | solution.py:27
  79.3 4.0 exponential_reduce_fusion.2
  84.2 4.0 exponential_reduce_fusion.2
  89.2 4.0 exponential_reduce_fusion.2
  94.1 4.0 exponential_reduce_fusion.2
  100.2 19.6 %while.35 = (s32[]{:T(128)}, f32[4,16,512]{2,1,0:T(8,128)S(1)}, bf16[4,512,128]{2,1,0:T(8,128)(2,1)S(1)}, bf16[1024,128]{1,0:T(8,128)(2,1)S(1)}, f32[16,64]{1,0:T(8,128)S(1)}, /*index=5*/s32[]{:T(128)}) while((s32[]{:T(128)}, f32[4,16,512]{2,1,0:T(8,128)S(1)}, bf16[4,512,128]{2,1,0:T(8,128)(2,1)S(1)}, bf16[1024,128]{1,0:T(8,128)(2,1)S(1)}, ...), condition=%wide.region_1.2_spmd, body=%wide.region_0.1_spmd.sunk | while | flops 141041664 | bytes 8884301 | solution.py:82
  100.2 1.7 maximum_bitcast_fusion.2
  101.9 1.9 copy.41
  105.1 1.7 maximum_bitcast_fusion.2
  106.8 1.9 copy.41
  110.0 1.7 maximum_bitcast_fusion.2
  111.7 1.9 copy.41
  114.8 1.7 maximum_bitcast_fusion.2
  116.6 1.9 copy.41
  120.0 24.4 %pmax.7 = f32[16]{0:T(128)S(1)} all-reduce(f32[16]{0:T(128)S(1)} %fusion.18), channel_id=1, replica_groups=mesh['context'=16,'heads'=16] {'context'}, use_global_device_ids=true, to_apply=%region_3.4 | all-reduce | flops 16 | bytes 128 | tf_op jit(solution)/shard_map/pmax | solution.py:85
  144.5 54.5 %all-reduce.3.cloned.1.call-done = f32[256,2048]{1,0:T(8,128)} async-done(((f32[256,2048]{1,0:T(8,128)}), f32[256,2048]{1,0:T(8,128)}) %all-reduce.3.cloned.1.call-update) | async-done | bytes 2097168 | tf_op jit(solution)/shard_map/psum | solution.py:53
  200.0 24.2 %all-reduce = (f32[16]{0:T(128)S(1)}, f32[16]{0:T(128)S(1)}) all-reduce(f32[16]{0:T(128)S(1)} %dynamic-slice_reduce_fusion, f32[16]{0:T(128)S(1)} %fusion.19), channel_id=1, replica_groups=mesh['context'=16,'heads'=16] {'context'}, use_global_device_ids=true, to_apply=%region_11.12 | all-reduce | flops 32 | bytes 256 | tf_op jit(solution)/shard_map/psum | solution.py:87
  226.0 27.1 %while.37 = (s32[]{:T(128)}, f32[1024,128]{1,0:T(8,128)S(1)}, f32[4,512,128]{2,1,0:T(8,128)}, bf16[4,512,128]{2,1,0:T(8,128)(2,1)S(1)}, bf16[1024,128]{1,0:T(8,1...) while((s32[]{:T(128)}, f32[1024,128]{1,0:T(8,128)S(1)}, ...), condition=%wide.wide.region_13.14_spmd.clone, body=%wide.wide.region_12.13_spmd.clone.sunk | while | flops 405536768 | bytes 13734523 | solution.py:107
  227.0 1.9 copy.42
  228.9 2.1 select_convert_fusion.3
  233.8 1.9 copy.42
  235.6 2.1 select_convert_fusion.3
  240.5 1.9 copy.42
  242.4 2.1 select_convert_fusion.3
  247.3 1.9 copy.42
  249.2 2.1 select_convert_fusion.3
  255.0 56.0 %reduce-scatter.3.cloned.1.call-done = f32[16,4,128]{2,0,1:T(8,128)} async-done(((f32[16,64,128]{2,0,1:T(8,128)}), f32[16,4,128]{2,0,1:T(8,128)}) %reduce-scatter.3.cloned.1.call-update) | async-done | bytes 32784 | tf_op jit(solution)/shard_map/reduce_scatter | solution.py:110
  310.9 1.4 copy.28
  312.3 80.0 %reduce-scatter.5.cloned.1.call-done = f32[128,128]{1,0:T(8,128)} async-done(((f32[2048,128]{1,0:T(8,128)}), f32[128,128]{1,0:T(8,128)}) %reduce-scatter.5.cloned.1.call-update) | async-done | bytes 65552 | tf_op jit(solution)/shard_map/reduce_scatter | solution.py:111
  (75 shorter events, 26.3 us)
Async XLA Ops:
  9.9 8.9 %copy-start.4 = (s32[256]{0:T(256)S(1)}, s32[256]{0:T(256)}, u32[]{:S(2)}) copy-start(s32[256]{0:T(256)} %param.16) | copy-start | bytes 3076
  9.9 9.0 %copy-start.3 = (f32[256,8]{0,1:T(8,128)S(1)}, f32[256,8]{0,1:T(8,128)}, u32[]{:S(2)}) copy-start(f32[256,8]{0,1:T(8,128)} %param.15) | copy-start | bytes 24580
  9.9 9.2 %copy-start.2 = (f32[16,64]{1,0:T(8,128)S(1)}, f32[16,64]{1,0:T(8,128)}, u32[]{:S(2)}) copy-start(f32[16,64]{1,0:T(8,128)} %param.19) | copy-start | bytes 12292
  9.9 69.4 %copy-start.5 = (bf16[2048,576]{0,1:T(8,128)(2,1)S(1)}, bf16[2048,576]{0,1:T(8,128)(2,1)}, u32[]{:S(2)}) copy-start(bf16[2048,576]{0,1:T(8,128)(2,1)} %param.14) | copy-start | bytes 7077892
  9.9 69.4 %all-to-all-start = ((bf16[16,16,8,576]{3,2,1,0:T(8,128)(2,1)}), bf16[16,16,8,576]{3,2,1,0:T(8,128)(2,1)}, u32[]{:S(2)}, u32[]{:S(2)}) async-start(bf16[16,16,8,576]{3,2,1,0:T(8,128)(2,1)} %stack.2), calls=%async_computation | async-start | bytes 5242880 | tf_op jit(solution)/shard_map/all_to_all | solution.py:45
  18.7 180.3 %all-reduce.3.cloned.1.call-start = ((), (), s32[]{:S(2)}) async-start(), calls=%async_computation.3 | async-start | bytes 4194304 | tf_op jit(solution)/shard_map/psum | solution.py:53
  99.0 0.9 copy-start
  99.0 1.1 copy-start.1
  99.1 211.9 %reduce-scatter.3.cloned.1.call-start = ((), (), s32[]{:S(2)}) async-start(), calls=%async_computation.4 | async-start | bytes 557056 | tf_op jit(solution)/shard_map/reduce_scatter | solution.py:110
  254.2 138.0 %reduce-scatter.5.cloned.1.call-start = ((), (), s32[]{:S(2)}) async-start(), calls=%async_computation.5 | async-start | bytes 1114112 | tf_op jit(solution)/shard_map/reduce_scatter | solution.py:111
Sparse Core Ops, SparseCore 0:
  99.2 99.7 all-reduce.2
  254.3 56.5 reduce-scatter.2
  315.0 77.2 reduce-scatter.4
